TPU v7x, 32 devices: a whole 2x2x4 slice. The times are simulated.
32 devices in a mesh: group: 4 (over y, x), member: 8 (over z, core).
Axes of the slice: x: 2, y: 2, z: 4, core: 2. Of those that a mesh axis runs over, the one named last changes fastest.
Arguments:
- factors: bfloat16 [4, 8192, 8192], P('group', 'member'), as said below
- owner: int32 [1], replicated, may hold values from 0 to 3
- grads: bfloat16 [8192, 512], P(None, 'group')
Outputs:
- new_factor: bfloat16 [8192, 8192], P('member', 'group')
Inputs may be any that keep to these rules, and one draw needn't show every extreme that they name: `owner`: index of the group that owns the updated factor. `factors`: every group's factor is upper triangular with a positive diagonal.
All inputs are finite; a program needn't handle non-finite values.
Results may differ from a plain program's by a relative error of at most 0.0061.
Values may be sent and summed in bfloat16 or wider, within the bound.
A program may use at most 192 MiB of HBM per device.

v0:
```python
import jax
import jax.numpy as jnp
from jax import lax
from jax.sharding import PartitionSpec as P

step_size = 1.0
highest = lax.Precision.HIGHEST


def from_root(value, axis, root):
    mine = lax.axis_index(axis) == root
    return lax.psum(jnp.where(mine, value, jnp.zeros_like(value)), axis)


def prefix(part, axis, combine, identity):
    count = lax.axis_size(axis)
    place = lax.axis_index(axis)
    ahead = count - 1 - place
    gathered = lax.all_gather(part, axis)
    state = jnp.zeros_like(part) + jnp.asarray(identity, part.dtype)

    def one(lap, state):
        source = count - 1 - lap
        return combine(state, lax.dynamic_index_in_dim(gathered, source, 0, False))

    return lax.fori_loop(0, ahead, one, state)


def contract_rows(left_block, right_block):
    return lax.dot_general(
        left_block, right_block, (((0,), (0,)), ((), ())), preferred_element_type=jnp.float32
    )


def add_blocks(earlier_sum, later_sum):
    return earlier_sum + later_sum


def shards(factors, owner, grads):
    local_panel = factors[0]
    factor_panel = from_root(local_panel, "group", owner[0])
    projected = jnp.dot(factor_panel, grads, preferred_element_type=jnp.float32).astype(
        jnp.bfloat16
    )
    precond = lax.psum_scatter(
        contract_rows(factor_panel, projected), "member", scatter_dimension=0, tiled=True
    ).astype(jnp.bfloat16)
    precond_wide = precond.astype(jnp.float32)
    square_total = lax.psum(jnp.sum(precond_wide * precond_wide), ("group", "member"))
    factor_order = factor_panel.shape[1]
    group_count = lax.axis_size("group")
    total_columns = precond.shape[1] * group_count
    mean_square = square_total / (factor_order * total_columns)
    step_rate = step_size / (1.0 + mean_square)
    block_width = factor_order // group_count
    group_index = lax.axis_index("group")
    own_block = lax.dynamic_slice_in_dim(factor_panel, group_index * block_width, block_width, 1)
    left_rows = lax.all_gather(precond, "group", axis=1, tiled=True)
    partial_terms = contract_rows(left_rows, own_block)
    tail_total = prefix(partial_terms, "member", add_blocks, jnp.zeros_like(partial_terms))
    diagonal_gram = jnp.triu(jnp.dot(left_rows, left_rows.T, preferred_element_type=jnp.float32))
    combined = jnp.dot(left_rows.astype(jnp.float32), tail_total, precision=highest)
    combined = combined + jnp.dot(diagonal_gram, own_block.astype(jnp.float32), precision=highest)
    updated = (1.0 + step_rate) * own_block.astype(
        jnp.float32
    ) - step_rate / total_columns * combined
    return updated.astype(jnp.bfloat16)


def solution(mesh):
    in_specs = (P("group", "member", None), P(), P(None, "group"))
    out_specs = P("member", "group")
    return jax.shard_map(shards, mesh=mesh, in_specs=in_specs, out_specs=out_specs, check_vma=False)
```

profile of v0, /device:TPU:0, one launch (start us, length us, event | category | flops | bytes accessed | tf_op | source)
XLA Modules:
  0.0 803.4 jit_solution(13536739586304521661)
XLA Ops:
  6.5 0.0 copy-start
  6.5 0.0 all-reduce.2.cloned.1.call-start
  7.3 6.6 select_bitcast_fusion
  13.9 0.0 all-reduce.2.cloned.1.call-update
  13.9 0.0 reduce-scatter.2.cloned.1.call-start
  14.0 316.4 %all-reduce.2.cloned.1.call-done = bf16[1024,8192]{1,0:T(8,128)(2,1)} async-done(((bf16[1024,8192]{1,0:T(8,128)(2,1)}), bf16[1024,8192]{1,0:T(8,128)(2,1)}) %all-reduce.2.cloned.1.call-update) | async-done | bytes 16777232 | tf_op jit(solution)/shard_map/psum | solution.py:12
  330.4 0.0 copy-done
  330.4 29.9 %fusion.10 = f32[8192,128]{1,0:T(8,128)} fusion(bf16[1024,8192]{1,0:T(8,128)(2,1)} %all-reduce.2.cloned.1.call-done, bf16[8192,128]{1,0:T(8,128)(2,1)S(1)} %copy-done), kind=kOutput, calls=%fused_computation.17 | convolution fusion | flops 4295098368 | bytes 23068672 | tf_op jit(solution)/shard_map/dot_general | solution.py:30
  360.3 0.0 reduce-scatter.2.cloned.1.call-update
  360.3 0.0 all-gather.4.cloned.1.call-start
  360.4 51.1 %reduce-scatter.2.cloned.1.call-done = f32[1024,128]{1,0:T(8,128)} async-done(((f32[8192,128]{1,0:T(8,128)}), f32[1024,128]{1,0:T(8,128)}) %reduce-scatter.2.cloned.1.call-update) | async-done | bytes 524304 | tf_op jit(solution)/shard_map/reduce_scatter | solution.py:45
  411.4 2.4 multiply_reduce_fusion
  413.9 0.0 all-gather.4.cloned.1.call-update
  413.9 0.0 all-gather.6.cloned.1.call-start
  414.0 24.9 %all-gather.4.cloned.1.call-done = bf16[1024,512]{1,0:T(8,128)(2,1)} async-done(((bf16[1024,128]{1,0:T(8,128)(2,1)}), bf16[1024,512]{1,0:T(8,128)(2,1)}) %all-gather.4.cloned.1.call-update) | async-done | bytes 1048592 | tf_op jit(solution)/shard_map/all_gather | solution.py:58
  438.9 6.9 fusion.3
  445.8 0.0 copy-start.2
  445.8 0.0 all-gather.6.cloned.1.call-update
  445.8 51.4 %psum.15 = f32[]{:T(128)} all-reduce(f32[]{:T(128)} %get-tuple-element.70), channel_id=1, replica_groups=mesh['group'=4,'member'=8] {'group','member'}, use_global_device_ids=true, to_apply=%region_3.4 | all-reduce | flops 1 | bytes 8 | tf_op jit(solution)/shard_map/psum | solution.py:49
  498.0 0.0 copy-done.2
  498.0 1.3 fusion.11
  499.3 17.2 %fusion = f32[1024,2048]{1,0:T(8,128)} fusion(f32[1024,1024]{1,0:T(8,128)S(1)} %fusion.11, bf16[1024,8192]{1,0:T(8,128)(2,1)} %all-reduce.2.cloned.1.call-done, s32[]{:T(128)S(6)} %select_n.28, s32[1024]{0:T(1024)S(1)} %iota_add_fusion), kind=kOutput, calls=%fused_computation.3 | convolution fusion | flops 25771900928 | bytes 16781316 | tf_op jit(solution)/shard_map/dot_general | solution.py:63
  516.5 219.1 %all-gather.6.cloned.1.call-done = f32[4096,2048]{1,0:T(8,128)} async-done(((f32[512,2048]{1,0:T(8,128)}), f32[4096,2048]{1,0:T(8,128)}) %all-gather.6.cloned.1.call-update) | async-done | bytes 33554448 | tf_op jit(solution)/shard_map/all_gather | solution.py:19
  735.6 2.4 broadcast_in_dim.11
  738.1 45.4 %while.12 = (s32[]{:T(128)}, f32[512,2048]{1,0:T(8,128)}, s32[]{:T(128)}, f32[8,512,2048]{2,1,0:T(8,128)}, s32[]{:T(128)}, /*index=5*/s32[]{:T(128)}, s32[]{:T(128)}, s32[]{:T(128)}) while((s32[]{:T(128)}, f32[512,2048]{1,0:T(8,128)}, s32[]{:T(128)}, f32[8,512,2048]{2,1,0:T(8,128)}, s32[]{:T(128)}, /*index=5*/s32[]{:T(128)}, s32[]{:T(128)}, ...), condition=%wide.region_5.6_spmd, body=%wide.region_4.5_spmd.sunk | while | flops 1048582 | bytes 12583047 | solution.py:26
  738.1 6.5 bitcast_add_fusion.2
  744.5 6.5 bitcast_add_fusion.2
  751.0 6.5 bitcast_add_fusion.2
  757.5 6.5 bitcast_add_fusion.2
  764.0 6.5 bitcast_add_fusion.2
  770.5 6.5 bitcast_add_fusion.2
  776.9 6.5 bitcast_add_fusion.2
  783.4 0.0 copy-start.1
  783.4 13.5 %subtract_convert_fusion = bf16[1024,2048]{1,0:T(8,128)(2,1)} fusion(f32[1024,2048]{1,0:T(8,128)} %fusion, f32[]{:T(128)S(6)} %div.11, f32[]{:T(128)S(6)} %add.47, bf16[1024,512]{1,0:T(8,128)(2,1)S(1)} %copy-done.2, f32[512,2048]{1,0:T(8,128)} %get-tuple-element.61, bf16[1024,8192]{1,0:T(8,128)(2,1)} %all-reduce.2.cloned.1.call-done, s32[]{:T(128)S(6)} %select_n.28), kind=kOutput, calls=%fused_computation.2 | convolution fusion | flops 12897484800 | bytes 22020108 | tf_op jit(solution)/shard_map/dot_general | solution.py:62
  796.9 0.0 copy-done.1
  (1 shorter events, 0.0 us)
Async XLA Ops:
  6.5 323.9 %copy-start = (bf16[8192,128]{1,0:T(8,128)(2,1)S(1)}, bf16[8192,128]{1,0:T(8,128)(2,1)}, u32[]{:S(2)}) copy-start(bf16[8192,128]{1,0:T(8,128)(2,1)} %param.7) | copy-start | bytes 6291460
  6.5 323.9 %all-reduce.2.cloned.1.call-start = ((), (), s32[]{:S(2)}) async-start(), calls=%async_computation.1 | async-start | bytes 33554432 | tf_op jit(solution)/shard_map/psum | solution.py:12
  13.9 397.5 %reduce-scatter.2.cloned.1.call-start = ((), (), s32[]{:S(2)}) async-start(), calls=%async_computation.2 | async-start | bytes 4718592 | tf_op jit(solution)/shard_map/reduce_scatter | solution.py:45
  360.3 78.6 %all-gather.4.cloned.1.call-start = ((), (), s32[]{:S(2)}) async-start(), calls=%async_computation.3 | async-start | bytes 1310720 | tf_op jit(solution)/shard_map/all_gather | solution.py:58
  413.9 321.7 %all-gather.6.cloned.1.call-start = ((), (), s32[]{:S(2)}) async-start(), calls=%async_computation.4 | async-start | bytes 37748736 | tf_op jit(solution)/shard_map/all_gather | solution.py:19
  445.8 52.2 %copy-start.2 = (bf16[1024,512]{1,0:T(8,128)(2,1)S(1)}, bf16[1024,512]{1,0:T(8,128)(2,1)}, u32[]{:S(2)}) copy-start(bf16[1024,512]{1,0:T(8,128)(2,1)} %all-gather.4.cloned.1.call-done) | copy-start | bytes 3145732
  783.4 13.5 %copy-start.1 = (bf16[8192,128]{1,0:T(8,128)(2,1)S(1)}, bf16[8192,128]{1,0:T(8,128)(2,1)}, u32[]{:S(2)}) copy-start(bf16[8192,128]{1,0:T(8,128)(2,1)} %param.7) | copy-start | bytes 6291460
Sparse Core Ops, SparseCore 0:
  14.1 316.3 all-reduce.1
  360.4 50.9 reduce-scatter.1
  414.0 24.8 all-gather.3
  445.9 289.6 all-gather.5
where the time goes:
time: 804 us; the launch traced here: 803 us
  waiting for transfers between devices  612 us (76%)
  matrix products  68.7 us (9%)
  other arithmetic  54.4 us (7%)
  blocking collectives  51.4 us (6%)
  between operations  14.7 us (2%)
    psum x1, waiting for transfers between devices, from_root(): return lax.psum(jnp.where(mine, value, jnp.zeros_like(value)), axis)  316 us
    all_gather x1, waiting for transfers between devices, prefix(): gathered = lax.all_gather(part, axis)  219 us
    psum x1, blocking collectives, shards(): lax.psum(jnp.sum(precond_wide * precond_wide), ('group', 'member'))  51.4 us
    reduce_scatter x1, waiting for transfers between devices, shards(): lax.psum_scatter(contract_rows(factor_panel, projected), 'member', scatte...  51.1 us
    add x7, other arithmetic, add_blocks(): return earlier_sum + later_sum  45.4 us
    dot_general x2, matrix products, contract_rows(): lax.dot_general(left_block, right_block, (((0,), (0,)), ((), ())), prefer...  36.8 us
    all_gather x1, waiting for transfers between devices, shards(): left_rows = lax.all_gather(precond, 'group', axis=1, tiled=True)  24.9 us
    dot_general x1, matrix products, shards(): jnp.dot(diagonal_gram, own_block.astype(jnp.float32), precision=highest)  17.2 us
  transfers between devices with their start and end apart: 4, of which 4 were waited for; matrix products, arithmetic and copies ran while one was open for 2% of the time, Pallas kernels for 0%

commit v1 on v0

v1 whole, which is shorter than its diff:
```python
import functools

import jax
import jax.numpy as jnp
from jax import lax
from jax.experimental import pallas as pl
from jax.experimental.pallas import tpu as pltpu
from jax.sharding import PartitionSpec as P

MESH = pl.DeviceIdType.MESH
step_size = 1.0


def serpentine(place):
    return (place // 2) * 2 + lax.rem(place + place // 2, 2)


def spread_kernel(root, groups, pieces, depth, f_ref, out_ref, stage, local_sem, send_sem, recv_sem):
    place = serpentine(lax.axis_index("group"))
    ahead = serpentine(lax.rem(place + 1, groups))
    behind = serpentine(lax.rem(place + groups - 1, groups))
    root_place = (root // 2) * 2 + (root + root // 2) % 2
    down = lax.rem(place - root_place + groups, groups)
    up = lax.rem(groups - down, groups)
    lanes = ((0, down, ahead), (1, up, behind))

    barrier = pltpu.get_barrier_semaphore()
    for neighbour in (ahead, behind):
        pl.semaphore_signal(barrier, inc=1, device_id={"group": neighbour}, device_id_type=MESH)
    pl.semaphore_wait(barrier, 2)

    def copy(source, side, piece, target):
        rows = pl.ds(pl.multiple_of((side * pieces + piece) * depth, depth), depth)
        return pltpu.make_async_remote_copy(
            src_ref=source.at[rows],
            dst_ref=out_ref.at[rows],
            send_sem=send_sem.at[side, piece],
            recv_sem=recv_sem.at[side, piece],
            device_id={"group": target},
            device_id_type=MESH,
        )

    @pl.when(down == 0)
    def _():
        @pl.loop(0, pieces)
        def _(piece):
            for side, _, target in lanes:
                copy(f_ref, side, piece, target).start()

        tall = stage.shape[0]

        @pl.loop(0, f_ref.shape[0] // tall)
        def _(block):
            rows = pl.ds(pl.multiple_of(block * tall, tall), tall)
            fetch = pltpu.make_async_copy(f_ref.at[rows], stage, local_sem.at[0])
            fetch.start()
            fetch.wait()
            store = pltpu.make_async_copy(stage, out_ref.at[rows], local_sem.at[1])
            store.start()
            store.wait()

        @pl.loop(0, pieces)
        def _(piece):
            for side, _, target in lanes:
                copy(f_ref, side, piece, target).wait_send()

    @pl.when(down > 0)
    def _():
        @pl.loop(0, pieces + groups - 2)
        def _(lap):
            for side, distance, target in lanes:
                piece = lap - distance + 1

                @pl.when((piece >= 0) & (piece < pieces))
                def _():
                    copy(out_ref, side, piece, target).wait_recv()

                    @pl.when(distance < groups - 1)
                    def _():
                        copy(out_ref, side, piece, target).start()

        @pl.loop(0, pieces)
        def _(piece):
            for side, distance, target in lanes:
                @pl.when(distance < groups - 1)
                def _():
                    copy(out_ref, side, piece, target).wait_send()


def spread(local_panel, owner, groups):
    rows, columns = local_panel.shape
    depth = 16
    pieces = rows // 2 // depth

    def branch(root, panel):
        return pl.pallas_call(
            functools.partial(spread_kernel, root, groups, pieces, depth),
            out_shape=jax.ShapeDtypeStruct((rows, columns), panel.dtype),
            in_specs=[pl.BlockSpec(memory_space=pl.ANY)],
            out_specs=pl.BlockSpec(memory_space=pl.ANY),
            scratch_shapes=[
                pltpu.VMEM((64, columns), panel.dtype),
                pltpu.SemaphoreType.DMA((2,)),
                pltpu.SemaphoreType.DMA((2, pieces)),
                pltpu.SemaphoreType.DMA((2, pieces)),
            ],
            compiler_params=pltpu.CompilerParams(
                collective_id=1 + root, has_side_effects=True, vmem_limit_bytes=4 * 2**20
            ),
            name=f"spread_{root}",
        )(panel)

    branches = [functools.partial(branch, root) for root in range(groups)]
    return lax.switch(owner, branches, local_panel)


def chain_kernel(
    members, pieces, term_ref, square_ref, tail_ref, total_ref,
    sibling, running, passed, given, other, slots,
    swap_send, swap_recv, run_send, run_recv, give_send, give_recv, square_send, square_recv,
):
    me = lax.axis_index("member")
    chip, core = me // 2, lax.rem(me, 2)
    chips = members // 2
    partner = chip * 2 + 1 - core
    below = lax.rem(me + members - 2, members)
    height, half = sibling.shape
    depth = height // pieces
    mine = pl.ds(pl.multiple_of(core * half, half), half)
    theirs = pl.ds(pl.multiple_of((1 - core) * half, half), half)

    barrier = pltpu.get_barrier_semaphore()
    for shift in range(1, members):
        pl.semaphore_signal(
            barrier, inc=1, device_id={"member": lax.rem(me + shift, members)}, device_id_type=MESH
        )
    pl.semaphore_wait(barrier, members - 1)

    def remote(source, target_ref, send, recv, target):
        return pltpu.make_async_remote_copy(
            src_ref=source, dst_ref=target_ref, send_sem=send, recv_sem=recv,
            device_id={"member": target}, device_id_type=MESH,
        )

    def rows_of(piece):
        return pl.ds(pl.multiple_of(piece * depth, depth), depth)

    def swap(piece):
        rows = rows_of(piece)
        return remote(
            term_ref.at[rows, theirs], sibling.at[rows], swap_send.at[piece], swap_recv.at[piece], partner
        )

    def run(piece):
        rows = rows_of(piece)
        return remote(passed.at[rows], running.at[rows], run_send.at[piece], run_recv.at[piece], below)

    def give(piece):
        rows = rows_of(piece)
        return remote(given.at[rows], other.at[rows], give_send.at[piece], give_recv.at[piece], partner)

    def square(shift, slot):
        return remote(
            square_ref, slots.at[slot], square_send.at[shift], square_recv.at[slot],
            lax.rem(me + shift, members),
        )

    @pl.loop(0, pieces)
    def _(piece):
        swap(piece).start()

    for shift in range(1, members):
        square(shift, me).start()

    @pl.when(chip == chips - 1)
    def _():
        running[...] = jnp.zeros_like(running)

    @pl.loop(0, pieces)
    def _(piece):
        rows = rows_of(piece)
        swap(piece).wait_recv()

        @pl.when(chip < chips - 1)
        def _():
            run(piece).wait_recv()

        late = running[rows, :].astype(jnp.float32)
        own = term_ref[rows, mine].astype(jnp.float32)
        beside = sibling[rows, :].astype(jnp.float32)

        @pl.when(chip > 0)
        def _():
            passed[rows, :] = (late + own + beside).astype(passed.dtype)
            run(piece).start()

        given[rows, :] = jnp.where(core == 1, late + own, late).astype(given.dtype)
        give(piece).start()
        tail_ref[rows, mine] = jnp.where(core == 0, late + beside, late).astype(tail_ref.dtype)

    @pl.loop(0, pieces)
    def _(piece):
        rows = rows_of(piece)
        give(piece).wait_recv()
        tail_ref[rows, theirs] = other[rows, :]
        swap(piece).wait_send()
        give(piece).wait_send()

        @pl.when(chip > 0)
        def _():
            run(piece).wait_send()

    total = square_ref[...]
    for shift in range(1, members):
        source = lax.rem(me + shift, members)
        square(shift, source).wait_recv()
        total = total + slots[source]
    total_ref[...] = total
    for shift in range(1, members):
        square(shift, me).wait_send()


def chain(term, squares, members, identifier):
    height, width = term.shape
    half = width // 2
    pieces = 8
    vmem = pl.BlockSpec(memory_space=pltpu.VMEM)
    buffer = pltpu.VMEM((height, half), term.dtype)
    sems = pltpu.SemaphoreType.DMA((pieces,))
    marks = pltpu.SemaphoreType.DMA((members,))
    return pl.pallas_call(
        functools.partial(chain_kernel, members, pieces),
        out_shape=(
            jax.ShapeDtypeStruct((height, width), term.dtype),
            jax.ShapeDtypeStruct(squares.shape, squares.dtype),
        ),
        in_specs=[vmem, vmem],
        out_specs=(vmem, vmem),
        scratch_shapes=[
            buffer, buffer, buffer, buffer, buffer,
            pltpu.VMEM((members, *squares.shape), squares.dtype),
            sems, sems, sems, sems, sems, sems, marks, marks,
        ],
        compiler_params=pltpu.CompilerParams(
            collective_id=identifier, has_side_effects=True, vmem_limit_bytes=32 * 2**20
        ),
        name="chain",
    )(term, squares)


def contract_rows(left_block, right_block):
    return lax.dot_general(
        left_block, right_block, (((0,), (0,)), ((), ())), preferred_element_type=jnp.float32
    )


def shards(groups, members, factors, owner, grads):
    factor_panel = spread(factors[0], owner[0], groups)
    projected = jnp.dot(factor_panel, grads, preferred_element_type=jnp.float32).astype(
        jnp.bfloat16
    )
    precond = lax.psum_scatter(
        contract_rows(factor_panel, projected), "member", scatter_dimension=0, tiled=True
    ).astype(jnp.bfloat16)
    factor_order = factor_panel.shape[1]
    total_columns = precond.shape[1] * groups
    block_width = factor_order // groups
    group_index = lax.axis_index("group")
    own_block = lax.dynamic_slice_in_dim(factor_panel, group_index * block_width, block_width, 1)
    left_rows = lax.all_gather(precond, "group", axis=1, tiled=True)
    left_wide = left_rows.astype(jnp.float32)
    squares = jnp.sum((left_wide * left_wide).reshape(-1, 8, left_wide.shape[1]), axis=0)
    terms = contract_rows(left_rows, own_block).astype(jnp.bfloat16)
    tail_total, square_sums = chain(terms, squares, members, groups + 1)
    diagonal_gram = jnp.triu(jnp.dot(left_rows, left_rows.T, preferred_element_type=jnp.float32))
    combined = jnp.dot(left_rows, tail_total, preferred_element_type=jnp.float32)
    combined = combined + jnp.dot(
        diagonal_gram.astype(jnp.bfloat16), own_block, preferred_element_type=jnp.float32
    )
    mean_square = jnp.sum(square_sums) / (factor_order * total_columns)
    step_rate = step_size / (1.0 + mean_square)
    updated = (1.0 + step_rate) * own_block.astype(
        jnp.float32
    ) - step_rate / total_columns * combined
    return updated.astype(jnp.bfloat16)


def solution(mesh):
    in_specs = (P("group", "member", None), P(), P(None, "group"))
    out_specs = P("member", "group")
    body = functools.partial(shards, mesh.shape["group"], mesh.shape["member"])
    return jax.shard_map(body, mesh=mesh, in_specs=in_specs, out_specs=out_specs, check_vma=False)
```

time: 804 us -> 391 us (0.49)
  waiting for transfers between devices: 612 us -> 76.5 us
  Pallas kernels: 0 us -> 238 us
  blocking collectives: 51.4 us -> 0 us
  other arithmetic: 54.4 us -> 3.86 us
  matrix products: 68.7 us -> 55.6 us
    psum x1 -> x0, waiting for transfers between devices: 316 us -> none  [from_root(): return lax.psum(jnp.where(mine, value, jnp.zeros_like(value)), axis)]
    pallas_call x0 -> x2, Pallas kernels: none -> 238 us  [the longest x1 199 us: branch(): pl.pallas_call(functools.partial(spread_kernel, root, groups, pieces, dep...]
    all_gather x1 -> x0, waiting for transfers between devices: 219 us -> none  [prefix(): gathered = lax.all_gather(part, axis)]
    psum x1 -> x0, blocking collectives: 51.4 us -> none  [shards(): lax.psum(jnp.sum(precond_wide * precond_wide), ('group', 'member'))]
    add x7 -> x0, other arithmetic: 45.4 us -> none  [add_blocks(): return earlier_sum + later_sum]
    dot_general x3 -> x2, matrix products: 32 us -> 20.8 us  [the longest x1 11.2 us: shards(): jnp.dot(diagonal_gram.astype(jnp.bfloat16), own_block, preferred_element_...]
  transfers between devices with their start and end apart: 4 -> 2, of which waited for: 4 -> 2; matrix products, arithmetic and copies ran while one was open for 2% -> 0% of each run, Pallas kernels for 0% -> 0%
where the time goes in v1:
time: 391 us; the launch traced here: 390 us
  Pallas kernels  238 us (61%)
  waiting for transfers between devices  76.5 us (20%)
  matrix products  55.6 us (14%)
  between operations  15 us (4%)
    pallas_call x1, Pallas kernels, branch(): pl.pallas_call(functools.partial(spread_kernel, root, groups, pieces, dep...  199 us
    reduce_scatter x1, waiting for transfers between devices, shards(): lax.psum_scatter(contract_rows(factor_panel, projected), 'member', scatte...  51.5 us
    pallas_call x1, Pallas kernels, chain(): pl.pallas_call(functools.partial(chain_kernel, members, pieces), out_shap...  39.2 us
    dot_general x2, matrix products, contract_rows(): lax.dot_general(left_block, right_block, (((0,), (0,)), ((), ())), prefer...  34.8 us
    all_gather x1, waiting for transfers between devices, shards(): left_rows = lax.all_gather(precond, 'group', axis=1, tiled=True)  25 us
    dot_general x1, matrix products, shards(): jnp.dot(diagonal_gram.astype(jnp.bfloat16), own_block, preferred_element_...  11.2 us
    dot_general x1, matrix products, shards(): jnp.dot(left_rows, tail_total, preferred_element_type=jnp.float32)  9.69 us
  transfers between devices with their start and end apart: 2, of which 2 were waited for; matrix products, arithmetic and copies ran while one was open for 0% of the time, Pallas kernels for 0%

profile of v1, /device:TPU:0, one launch (start us, length us, event | category | flops | bytes accessed | tf_op | source)
XLA Modules:
  0.0 390.4 jit_solution(7458677384778771707)
XLA Ops:
  6.5 0.0 copy-start
  6.5 0.0 reduce-scatter.2.cloned.1.call-start
  7.3 198.9 %conditional.1 = (bf16[1024,8192]{1,0:T(8,128)(2,1)}) conditional(s32[]{:T(128)} %bitcast, bf16[1024,8192]{1,0:T(8,128)(2,1)} %bitcast.21, bf16[1024,8192]{1,0:T(8,128)(2,1)} %bitcast.22, bf16[1024,8192]{1,0:T(8,128)(2,1)} %bitcast.23, bf16[1024,8192]{1,0:T(8,128)(2,1)} %bitcast.24), branch_computations={%region_0.0_spmd, %region_1.0_spmd, %region_2.0_spmd, %region_3.0_... | conditional | bytes 8 | solution.py:114
  7.4 198.8 %spread_3.1 = bf16[1024,8192]{1,0:T(8,128)(2,1)} custom-call(bf16[1024,8192]{1,0:T(8,128)(2,1)} %f_ref.3), custom_call_target="tpu_custom_call" | custom-call | tf_op jit(solution)/shard_map/cond/branch_3_fun/spread_3/pallas_call | solution.py:96
  206.2 0.0 copy-done
  206.2 29.8 %fusion.10 = f32[8192,128]{1,0:T(8,128)} fusion(bf16[1024,8192]{1,0:T(8,128)(2,1)} %get-tuple-element.18, bf16[8192,128]{1,0:T(8,128)(2,1)S(1)} %copy-done), kind=kOutput, calls=%fused_computation.14 | convolution fusion | flops 4295098368 | bytes 23068672 | tf_op jit(solution)/shard_map/dot_general | solution.py:252
  236.1 0.0 reduce-scatter.2.cloned.1.call-update
  236.1 0.0 all-gather.2.cloned.1.call-start
  236.1 51.5 %reduce-scatter.2.cloned.1.call-done = f32[1024,128]{1,0:T(8,128)} async-done(((f32[8192,128]{1,0:T(8,128)}), f32[1024,128]{1,0:T(8,128)}) %reduce-scatter.2.cloned.1.call-update) | async-done | bytes 524304 | tf_op jit(solution)/shard_map/reduce_scatter | solution.py:262
  287.6 1.8 convert_element_type.22
  289.4 0.0 all-gather.2.cloned.1.call-update
  289.4 25.0 %all-gather.2.cloned.1.call-done = bf16[1024,512]{1,0:T(8,128)(2,1)} async-done(((bf16[1024,128]{1,0:T(8,128)(2,1)}), bf16[1024,512]{1,0:T(8,128)(2,1)}) %all-gather.2.cloned.1.call-update) | async-done | bytes 1048592 | tf_op jit(solution)/shard_map/all_gather | solution.py:270
  314.4 1.5 bitcast_reduce_fusion.square_ref
  315.9 0.0 copy-start.2
  315.9 5.0 %fusion.4.term_ref = bf16[512,2048]{1,0:T(8,128)(2,1)S(1)} fusion(bf16[1024,512]{1,0:T(8,128)(2,1)} %all-gather.2.cloned.1.call-done, bf16[1024,8192]{1,0:T(8,128)(2,1)} %get-tuple-element.18, s32[]{:T(128)S(6)} %select_n.7), kind=kOutput, calls=%fused_computation.7 | convolution fusion | flops 2148532224 | bytes 7340036 | tf_op jit(solution)/shard_map/dot_general | solution.py:252
  320.9 39.2 %chain.1 = (bf16[512,2048]{1,0:T(8,128)(2,1)S(1)}, f32[8,512]{1,0:T(8,128)S(1)}) custom-call(bf16[512,2048]{1,0:T(8,128)(2,1)S(1)} %fusion.4.term_ref, f32[8,512]{1,0:T(8,128)S(1)} %bitcast_reduce_fusion.square_ref), custom_call_target="tpu_custom_call" | custom-call | tf_op jit(solution)/shard_map/chain/pallas_call | solution.py:231
  360.0 0.0 copy-start.1
  360.0 1.4 copy-done.1
  361.4 0.6 reduce_sum.19
  362.7 0.0 copy-done.2
  362.7 11.2 %fusion = f32[1024,2048]{1,0:T(8,128)} fusion(bf16[1024,8192]{1,0:T(8,128)(2,1)} %get-tuple-element.18, s32[]{:T(128)S(6)} %select_n.7, bf16[1024,512]{1,0:T(8,128)(2,1)S(1)} %copy-done.2, s32[1024]{0:T(1024)S(1)} %iota_add_fusion), kind=kOutput, calls=%fused_computation.3 | convolution fusion | flops 5371854848 | bytes 14684164 | tf_op jit(solution)/shard_map/dot_general | solution.py:277
  373.9 9.7 %subtract_convert_fusion = bf16[1024,2048]{1,0:T(8,128)(2,1)} fusion(f32[1024,2048]{1,0:T(8,128)} %fusion, f32[]{:T(128)S(6)} %div.11, f32[]{:T(128)S(6)} %add.25, bf16[1024,512]{1,0:T(8,128)(2,1)S(1)} %copy-done.2, bf16[512,2048]{1,0:T(8,128)(2,1)} %copy-done.1, bf16[1024,8192]{1,0:T(8,128)(2,1)} %get-tuple-element.18, s32[]{:T(128)S(6)} %select_n.7), kind=kOutput, calls=%fused_computation | convolution fusion | flops 2160066560 | bytes 19922956 | tf_op jit(solution)/shard_map/dot_general | solution.py:276
  (1 shorter events, 0.0 us)
Async XLA Ops:
  6.5 199.7 %copy-start = (bf16[8192,128]{1,0:T(8,128)(2,1)S(1)}, bf16[8192,128]{1,0:T(8,128)(2,1)}, u32[]{:S(2)}) copy-start(bf16[8192,128]{1,0:T(8,128)(2,1)} %param.9) | copy-start | bytes 6291460
  6.5 281.1 %reduce-scatter.2.cloned.1.call-start = ((), (), s32[]{:S(2)}) async-start(), calls=%async_computation.1 | async-start | bytes 4718592 | tf_op jit(solution)/shard_map/reduce_scatter | solution.py:262
  236.1 78.3 %all-gather.2.cloned.1.call-start = ((), (), s32[]{:S(2)}) async-start(), calls=%async_computation.2 | async-start | bytes 1310720 | tf_op jit(solution)/shard_map/all_gather | solution.py:270
  315.9 46.8 %copy-start.2 = (bf16[1024,512]{1,0:T(8,128)(2,1)S(1)}, bf16[1024,512]{1,0:T(8,128)(2,1)}, u32[]{:S(2)}) copy-start(bf16[1024,512]{1,0:T(8,128)(2,1)} %all-gather.2.cloned.1.call-done) | copy-start | bytes 3145732
  360.0 1.4 copy-start.1
Sparse Core Ops, SparseCore 0:
  236.2 51.3 reduce-scatter.1
  289.5 24.8 all-gather.1

commit v2 on v1

--- a/solution.py
+++ b/solution.py
@@ -15,7 +15,20 @@
     return (place // 2) * 2 + lax.rem(place + place // 2, 2)
 
 
-def spread_kernel(root, groups, pieces, depth, f_ref, out_ref, stage, local_sem, send_sem, recv_sem):
+def spread_kernel(
+    root, groups, members, tall, f_ref, out_ref, aid_ref, stage, local_sem, zero_sem,
+    send_sem, recv_sem, lend_send, lend_recv, aid_send, aid_recv, home_send, home_recv,
+):
+    rows, columns = f_ref.shape
+    chips = members // 2
+    wide = columns // chips
+    blocks = rows // tall
+    lent = blocks // 4
+    me = lax.axis_index("member")
+    chip = me // 2
+    first, last = chip == 0, chip == chips - 1
+    far = lax.rem(me + members - 2, members)
+    near = lax.rem(me + 2, members)
     place = serpentine(lax.axis_index("group"))
     ahead = serpentine(lax.rem(place + 1, groups))
     behind = serpentine(lax.rem(place + groups - 1, groups))
@@ -23,92 +36,232 @@
     down = lax.rem(place - root_place + groups, groups)
     up = lax.rem(groups - down, groups)
     lanes = ((0, down, ahead), (1, up, behind))
+    lent_side, full_side, short_side = lent // 2, blocks // 2, (blocks - lent) // 2
+    count = jnp.where(first, short_side * chips, full_side * (chips - chip))
 
     barrier = pltpu.get_barrier_semaphore()
     for neighbour in (ahead, behind):
         pl.semaphore_signal(barrier, inc=1, device_id={"group": neighbour}, device_id_type=MESH)
-    pl.semaphore_wait(barrier, 2)
-
-    def copy(source, side, piece, target):
-        rows = pl.ds(pl.multiple_of((side * pieces + piece) * depth, depth), depth)
+
+    @pl.when(first)
+    def _():
+        pl.semaphore_signal(barrier, inc=1, device_id={"member": far}, device_id_type=MESH)
+
+    @pl.when(last)
+    def _():
+        pl.semaphore_signal(barrier, inc=1, device_id={"member": near}, device_id_type=MESH)
+
+    pl.semaphore_wait(barrier, 2 + jnp.where(first | last, 1, 0))
+
+    def window(row, column):
+        return (
+            pl.ds(pl.multiple_of(row * tall, tall), tall),
+            pl.ds(pl.multiple_of(column * wide, wide), wide),
+        )
+
+    def own(source, side, piece, target):
+        row = jnp.where(
+            first,
+            side * short_side + piece % short_side,
+            side * full_side + piece % full_side,
+        )
+        column = jnp.where(first, piece // short_side, chip + piece // full_side)
+        spot = window(row, column)
         return pltpu.make_async_remote_copy(
-            src_ref=source.at[rows],
-            dst_ref=out_ref.at[rows],
-            send_sem=send_sem.at[side, piece],
-            recv_sem=recv_sem.at[side, piece],
-            device_id={"group": target},
-            device_id_type=MESH,
-        )
+            src_ref=source.at[spot], dst_ref=out_ref.at[spot],
+            send_sem=send_sem.at[side, piece], recv_sem=recv_sem.at[side, piece],
+            device_id={"group": target}, device_id_type=MESH,
+        )
+
+    def lent_spot(side, piece):
+        return side * lent_side + piece % lent_side, piece // lent_side
+
+    def lend(side, piece):
+        row, column = lent_spot(side, piece)
+        return pltpu.make_async_remote_copy(
+            src_ref=f_ref.at[window(blocks - lent + row, column)],
+            dst_ref=aid_ref.at[window(row, column)],
+            send_sem=lend_send.at[side, piece], recv_sem=lend_recv.at[side, piece],
+            device_id={"member": far}, device_id_type=MESH,
+        )
+
+    def aid(side, piece, target):
+        spot = window(*lent_spot(side, piece))
+        return pltpu.make_async_remote_copy(
+            src_ref=aid_ref.at[spot], dst_ref=aid_ref.at[spot],
+            send_sem=aid_send.at[side, piece], recv_sem=aid_recv.at[side, piece],
+            device_id={"group": target}, device_id_type=MESH,
+        )
+
+    def home(side, piece):
+        row, column = lent_spot(side, piece)
+        return pltpu.make_async_remote_copy(
+            src_ref=aid_ref.at[window(row, column)],
+            dst_ref=out_ref.at[window(blocks - lent + row, column)],
+            send_sem=home_send.at[side, piece], recv_sem=home_recv.at[side, piece],
+            device_id={"member": near}, device_id_type=MESH,
+        )
+
+    lent_count = lent_side * chips
 
     @pl.when(down == 0)
     def _():
-        @pl.loop(0, pieces)
+        @pl.when(first)
+        def _():
+            @pl.loop(0, lent_count)
+            def _(piece):
+                for side in (0, 1):
+                    lend(side, piece).start()
+
+        @pl.loop(0, count)
         def _(piece):
             for side, _, target in lanes:
-                copy(f_ref, side, piece, target).start()
-
-        tall = stage.shape[0]
-
-        @pl.loop(0, f_ref.shape[0] // tall)
-        def _(block):
-            rows = pl.ds(pl.multiple_of(block * tall, tall), tall)
-            fetch = pltpu.make_async_copy(f_ref.at[rows], stage, local_sem.at[0])
+                own(f_ref, side, piece, target).start()
+
+        @pl.when(last)
+        def _():
+            @pl.loop(0, lent_count)
+            def _(piece):
+                for side, _, target in lanes:
+                    lend(side, piece).wait_recv()
+                    aid(side, piece, target).start()
+
+        @pl.loop(0, chips)
+        def _(column):
+            lanes_of = pl.ds(pl.multiple_of(column * wide, wide), wide)
+            fetch = pltpu.make_async_copy(f_ref.at[:, lanes_of], stage, local_sem.at[0])
             fetch.start()
             fetch.wait()
-            store = pltpu.make_async_copy(stage, out_ref.at[rows], local_sem.at[1])
+            store = pltpu.make_async_copy(stage, out_ref.at[:, lanes_of], local_sem.at[1])
             store.start()
             store.wait()
 
-        @pl.loop(0, pieces)
+        @pl.loop(0, count)
         def _(piece):
             for side, _, target in lanes:
-                copy(f_ref, side, piece, target).wait_send()
+                own(f_ref, side, piece, target).wait_send()
+
+        @pl.when(first)
+        def _():
+            @pl.loop(0, lent_count)
+            def _(piece):
+                for side in (0, 1):
+                    lend(side, piece).wait_send()
+
+        @pl.when(last)
+        def _():
+            @pl.loop(0, lent_count)
+            def _(piece):
+                for side, _, target in lanes:
+                    aid(side, piece, target).wait_send()
 
     @pl.when(down > 0)
     def _():
-        @pl.loop(0, pieces + groups - 2)
+        def blank(column):
+            lanes_of = pl.ds(pl.multiple_of(column * wide, wide), wide)
+            return pltpu.make_async_copy(stage, out_ref.at[:, lanes_of], zero_sem.at[column])
+
+        @pl.when(chip > 0)
+        def _():
+            @pl.loop(0, blocks)
+            def _(block):
+                part = pl.ds(pl.multiple_of(block * tall, tall), tall)
+                stage[part, :] = jnp.zeros((tall, wide), stage.dtype)
+
+            @pl.loop(0, chip)
+            def _(column):
+                blank(column).start()
+
+        @pl.loop(0, count + groups - 2)
         def _(lap):
             for side, distance, target in lanes:
                 piece = lap - distance + 1
 
-                @pl.when((piece >= 0) & (piece < pieces))
+                @pl.when((piece >= 0) & (piece < count))
                 def _():
-                    copy(out_ref, side, piece, target).wait_recv()
+                    own(out_ref, side, piece, target).wait_recv()
 
                     @pl.when(distance < groups - 1)
                     def _():
-                        copy(out_ref, side, piece, target).start()
-
-        @pl.loop(0, pieces)
+                        own(out_ref, side, piece, target).start()
+
+        @pl.when(last)
+        def _():
+            @pl.loop(0, lent_count + groups - 2)
+            def _(lap):
+                for side, distance, target in lanes:
+                    piece = lap - distance + 1
+
+                    @pl.when((piece >= 0) & (piece < lent_count))
+                    def _():
+                        aid(side, piece, target).wait_recv()
+
+                        @pl.when(distance < groups - 1)
+                        def _():
+                            aid(side, piece, target).start()
+
+                        home(side, piece).start()
+
+        @pl.when(first)
+        def _():
+            @pl.loop(0, lent_count)
+            def _(piece):
+                for side in (0, 1):
+                    home(side, piece).wait_recv()
+
+        @pl.loop(0, count)
         def _(piece):
             for side, distance, target in lanes:
                 @pl.when(distance < groups - 1)
                 def _():
-                    copy(out_ref, side, piece, target).wait_send()
-
-
-def spread(local_panel, owner, groups):
+                    own(out_ref, side, piece, target).wait_send()
+
+        @pl.when(last)
+        def _():
+            @pl.loop(0, lent_count)
+            def _(piece):
+                for side, distance, target in lanes:
+                    home(side, piece).wait_send()
+
+                    @pl.when(distance < groups - 1)
+                    def _():
+                        aid(side, piece, target).wait_send()
+
+        @pl.loop(0, chip)
+        def _(column):
+            blank(column).wait()
+
+
+def spread(local_panel, owner, groups, members):
     rows, columns = local_panel.shape
-    depth = 16
-    pieces = rows // 2 // depth
+    tall = 64
+    chips = members // 2
+    blocks = rows // tall
+    lent = blocks // 4
+    most = max((blocks - lent) // 2 * chips, blocks // 2 * (chips - 1))
+    ring = pltpu.SemaphoreType.DMA((2, most))
+    extra = pltpu.SemaphoreType.DMA((2, lent // 2 * chips))
 
     def branch(root, panel):
         return pl.pallas_call(
-            functools.partial(spread_kernel, root, groups, pieces, depth),
-            out_shape=jax.ShapeDtypeStruct((rows, columns), panel.dtype),
+            functools.partial(spread_kernel, root, groups, members, tall),
+            out_shape=(
+                jax.ShapeDtypeStruct((rows, columns), panel.dtype),
+                jax.ShapeDtypeStruct((lent * tall, columns), panel.dtype),
+            ),
             in_specs=[pl.BlockSpec(memory_space=pl.ANY)],
-            out_specs=pl.BlockSpec(memory_space=pl.ANY),
+            out_specs=(pl.BlockSpec(memory_space=pl.ANY), pl.BlockSpec(memory_space=pl.ANY)),
             scratch_shapes=[
-                pltpu.VMEM((64, columns), panel.dtype),
+                pltpu.VMEM((rows, columns // chips), panel.dtype),
                 pltpu.SemaphoreType.DMA((2,)),
-                pltpu.SemaphoreType.DMA((2, pieces)),
-                pltpu.SemaphoreType.DMA((2, pieces)),
+                pltpu.SemaphoreType.DMA((chips,)),
+                ring, ring, extra, extra, extra, extra, extra, extra,
             ],
             compiler_params=pltpu.CompilerParams(
-                collective_id=1 + root, has_side_effects=True, vmem_limit_bytes=4 * 2**20
+                collective_id=1 + root, has_side_effects=True, vmem_limit_bytes=12 * 2**20
             ),
             name=f"spread_{root}",
-        )(panel)
+        )(panel)[0]
 
     branches = [functools.partial(branch, root) for root in range(groups)]
     return lax.switch(owner, branches, local_panel)
@@ -255,25 +408,28 @@
 
 
 def shards(groups, members, factors, owner, grads):
-    factor_panel = spread(factors[0], owner[0], groups)
+    factor_panel = spread(factors[0], owner[0], groups, members)
     projected = jnp.dot(factor_panel, grads, preferred_element_type=jnp.float32).astype(
         jnp.bfloat16
     )
-    precond = lax.psum_scatter(
-        contract_rows(factor_panel, projected), "member", scatter_dimension=0, tiled=True
-    ).astype(jnp.bfloat16)
+    partial_rows = contract_rows(projected, factor_panel)
+    width = partial_rows.shape[0]
+    split_rows = partial_rows.reshape(width, members, -1).transpose(1, 0, 2)
+    precond = lax.psum_scatter(split_rows, "member", scatter_dimension=0, tiled=True)[0].astype(
+        jnp.bfloat16
+    )
     factor_order = factor_panel.shape[1]
-    total_columns = precond.shape[1] * groups
+    total_columns = width * groups
     block_width = factor_order // groups
     group_index = lax.axis_index("group")
     own_block = lax.dynamic_slice_in_dim(factor_panel, group_index * block_width, block_width, 1)
-    left_rows = lax.all_gather(precond, "group", axis=1, tiled=True)
+    left_rows = lax.all_gather(precond, "group", axis=0, tiled=True)
     left_wide = left_rows.astype(jnp.float32)
     squares = jnp.sum((left_wide * left_wide).reshape(-1, 8, left_wide.shape[1]), axis=0)
-    terms = contract_rows(left_rows, own_block).astype(jnp.bfloat16)
+    terms = jnp.dot(left_rows, own_block, preferred_element_type=jnp.float32).astype(jnp.bfloat16)
     tail_total, square_sums = chain(terms, squares, members, groups + 1)
-    diagonal_gram = jnp.triu(jnp.dot(left_rows, left_rows.T, preferred_element_type=jnp.float32))
-    combined = jnp.dot(left_rows, tail_total, preferred_element_type=jnp.float32)
+    diagonal_gram = jnp.triu(contract_rows(left_rows, left_rows))
+    combined = contract_rows(left_rows, tail_total)
     combined = combined + jnp.dot(
         diagonal_gram.astype(jnp.bfloat16), own_block, preferred_element_type=jnp.float32
     )

time: 391 us -> 353 us (0.903)
  Pallas kernels: 238 us -> 206 us
  matrix products: 55.6 us -> 50 us
  waiting for transfers between devices: 76.5 us -> 71 us
  local copies, waits for them, and re-layouts: 1.37 us -> 6.07 us
    pallas_call x1, Pallas kernels: 199 us -> 165 us  [branch(): pl.pallas_call(functools.partial(spread_kernel, root, groups, members, ta...]
    reduce_scatter x1, waiting for transfers between devices: 51.5 us -> 45.9 us  [shards(): lax.psum_scatter(split_rows, 'member', scatter_dimension=0, tiled=True)[0]]
    dot_general x1, matrix products: 9.69 us -> 4.93 us  [shards(): jnp.dot(left_rows, own_block, preferred_element_type=jnp.float32)]
    reshape x0 -> x1, local copies, waits for them, and re-layouts: none -> 4.71 us  [shards(): split_rows = partial_rows.reshape(width, members, -1).transpose(1, 0, 2)]
where the time goes in v2:
time: 353 us; the launch traced here: 352 us
  Pallas kernels  206 us (58%)
  waiting for transfers between devices  71 us (20%)
  matrix products  50 us (14%)
  between operations  15 us (4%)
  local copies, waits for them, and re-layouts  6.07 us (2%)
  other arithmetic  3.85 us (1%)
    pallas_call x1, Pallas kernels, branch(): pl.pallas_call(functools.partial(spread_kernel, root, groups, members, ta...  165 us
    reduce_scatter x1, waiting for transfers between devices, shards(): lax.psum_scatter(split_rows, 'member', scatter_dimension=0, tiled=True)[0]  45.9 us
    pallas_call x1, Pallas kernels, chain(): pl.pallas_call(functools.partial(chain_kernel, members, pieces), out_shap...  41.3 us
    dot_general x2, matrix products, contract_rows(): lax.dot_general(left_block, right_block, (((0,), (0,)), ((), ())), prefer...  33.9 us
    all_gather x1, waiting for transfers between devices, shards(): left_rows = lax.all_gather(precond, 'group', axis=0, tiled=True)  25.1 us
    dot_general x1, matrix products, shards(): jnp.dot(diagonal_gram.astype(jnp.bfloat16), own_block, preferred_element_...  11.2 us
  transfers between devices with their start and end apart: 2, of which 2 were waited for; matrix products, arithmetic and copies ran while one was open for 0% of the time, Pallas kernels for 0%

profile of v2, /device:TPU:0, one launch (start us, length us, event | category | flops | bytes accessed | tf_op | source)
XLA Modules:
  0.0 352.2 jit_solution(6282434821480807163)
XLA Ops:
  6.5 0.0 copy-start
  6.5 0.0 reduce-scatter.2.cloned.1.call-start
  7.3 165.0 %conditional.1 = (bf16[1024,8192]{1,0:T(8,128)(2,1)}) conditional(s32[]{:T(128)} %bitcast, bf16[1024,8192]{1,0:T(8,128)(2,1)} %bitcast.24, bf16[1024,8192]{1,0:T(8,128)(2,1)} %bitcast.25, bf16[1024,8192]{1,0:T(8,128)(2,1)} %bitcast.26, bf16[1024,8192]{1,0:T(8,128)(2,1)} %bitcast.27), branch_computations={%region_0.0_spmd, %region_1.0_spmd, %region_2.0_spmd, %region_3.0_... | conditional | bytes 8 | solution.py:267
  7.4 165.0 %spread_3.1 = (bf16[1024,8192]{1,0:T(8,128)(2,1)}, bf16[256,8192]{1,0:T(8,128)(2,1)}) custom-call(bf16[1024,8192]{1,0:T(8,128)(2,1)} %f_ref.3), custom_call_target="tpu_custom_call" | custom-call | tf_op jit(solution)/shard_map/cond/branch_3_fun/spread_3/pallas_call | solution.py:246
  172.4 0.0 copy-done
  172.4 23.5 %fusion.7 = f32[128,8192]{1,0:T(8,128)} fusion(bf16[1024,8192]{1,0:T(8,128)(2,1)} %get-tuple-element.22, bf16[8192,128]{1,0:T(8,128)(2,1)S(1)} %copy-done), kind=kOutput, calls=%fused_computation.11 | convolution fusion | flops 4295098368 | bytes 23068672 | tf_op jit(solution)/shard_map/dot_general | solution.py:405
  195.9 4.7 %copy.7 = f32[16,8,8,1024]{3,2,0,1:T(8,128)} copy(f32[16,8,8,1024]{3,2,1,0:T(8,128)} %bitcast.28) | data formatting | bytes 8388608 | tf_op jit(solution)/shard_map/reshape | solution.py:417
  200.6 0.0 reduce-scatter.2.cloned.1.call-update
  200.6 0.0 all-gather.3.cloned.1.call-start
  200.7 45.9 %reduce-scatter.2.cloned.1.call-done = f32[1,128,1024]{2,1,0:T(8,128)} async-done(((f32[8,128,1024]{2,1,0:T(8,128)}), f32[1,128,1024]{2,1,0:T(8,128)}) %reduce-scatter.2.cloned.1.call-update) | async-done | bytes 524304 | tf_op jit(solution)/shard_map/reduce_scatter | solution.py:418
  246.5 1.8 convert_element_type.25
  248.3 0.0 all-gather.3.cloned.1.call-update
  248.4 25.1 %all-gather.3.cloned.1.call-done = bf16[1,512,1024]{2,1,0:T(8,128)(2,1)} async-done(((bf16[1,128,1024]{2,1,0:T(8,128)(2,1)}), bf16[1,512,1024]{2,1,0:T(8,128)(2,1)}) %all-gather.3.cloned.1.call-update) | async-done | bytes 1048592 | tf_op jit(solution)/shard_map/all_gather | solution.py:426
  273.5 1.5 bitcast_reduce_fusion.square_ref
  274.9 0.0 copy-start.3
  274.9 4.9 %fusion.4.term_ref = bf16[512,2048]{1,0:T(8,128)(2,1)S(1)} fusion(bf16[1024,8192]{1,0:T(8,128)(2,1)} %get-tuple-element.22, s32[]{:T(128)S(6)} %select_n.7, bf16[1,512,1024]{2,1,0:T(8,128)(2,1)} %all-gather.3.cloned.1.call-done), kind=kOutput, calls=%fused_computation.8 | convolution fusion | flops 2148532224 | bytes 7340036 | tf_op jit(solution)/shard_map/dot_general | solution.py:429
  279.9 41.3 %chain.1 = (bf16[512,2048]{1,0:T(8,128)(2,1)S(1)}, f32[8,1024]{1,0:T(8,128)S(1)}) custom-call(bf16[512,2048]{1,0:T(8,128)(2,1)S(1)} %fusion.4.term_ref, f32[8,1024]{1,0:T(8,128)S(1)} %bitcast_reduce_fusion.square_ref), custom_call_target="tpu_custom_call" | custom-call | tf_op jit(solution)/shard_map/chain/pallas_call | solution.py:384
  321.2 0.0 copy-start.2
  321.2 1.3 copy-done.2
  322.5 0.6 reduce_sum.19
  323.8 0.0 copy-done.3
  323.9 11.2 %fusion = f32[1024,2048]{1,0:T(8,128)} fusion(bf16[1024,8192]{1,0:T(8,128)(2,1)} %get-tuple-element.22, s32[]{:T(128)S(6)} %select_n.7, s32[1024]{0:T(1024)S(1)} %iota_add_fusion, bf16[1,512,1024]{2,1,0:T(8,128)(2,1)S(1)} %copy-done.3), kind=kOutput, calls=%fused_computation.4 | convolution fusion | flops 5371854848 | bytes 13635588 | tf_op jit(solution)/shard_map/dot_general | solution.py:433
  335.0 0.0 copy-start.1
  335.0 10.4 %subtract_convert_fusion = bf16[1024,2048]{1,0:T(8,128)(2,1)} fusion(f32[1024,2048]{1,0:T(8,128)} %fusion, f32[]{:T(128)S(6)} %div.11, f32[]{:T(128)S(6)} %add.25, bf16[512,2048]{1,0:T(8,128)(2,1)} %copy-done.2, bf16[1024,8192]{1,0:T(8,128)(2,1)} %get-tuple-element.22, s32[]{:T(128)S(6)} %select_n.7, bf16[1,512,1024]{2,1,0:T(8,128)(2,1)S(1)} %copy-done.3), kind=kOutput, calls=%fused_computation | convolution fusion | flops 2160066560 | bytes 19922956 | tf_op jit(solution)/shard_map/dot_general | solution.py:405
  345.4 0.0 copy-done.1
  (1 shorter events, 0.0 us)
Async XLA Ops:
  6.5 165.8 %copy-start = (bf16[8192,128]{1,0:T(8,128)(2,1)S(1)}, bf16[8192,128]{1,0:T(8,128)(2,1)}, u32[]{:S(2)}) copy-start(bf16[8192,128]{1,0:T(8,128)(2,1)} %param.9) | copy-start | bytes 6291460
  6.5 240.0 %reduce-scatter.2.cloned.1.call-start = ((), (), s32[]{:S(2)}) async-start(), calls=%async_computation.1 | async-start | bytes 4718592 | tf_op jit(solution)/shard_map/reduce_scatter | solution.py:418
  200.6 72.9 %all-gather.3.cloned.1.call-start = ((), (), s32[]{:S(2)}) async-start(), calls=%async_computation.2 | async-start | bytes 1310720 | tf_op jit(solution)/shard_map/all_gather | solution.py:426
  274.9 48.9 %copy-start.3 = (bf16[1,512,1024]{2,1,0:T(8,128)(2,1)S(1)}, bf16[1,512,1024]{2,1,0:T(8,128)(2,1)}, u32[]{:S(2)}) copy-start(bf16[1,512,1024]{2,1,0:T(8,128)(2,1)} %all-gather.3.cloned.1.call-done) | copy-start | bytes 3145732
  321.2 1.4 copy-start.2
  335.0 10.4 %copy-start.1 = (bf16[8192,128]{1,0:T(8,128)(2,1)S(1)}, bf16[8192,128]{1,0:T(8,128)(2,1)}, u32[]{:S(2)}) copy-start(bf16[8192,128]{1,0:T(8,128)(2,1)} %param.9) | copy-start | bytes 6291460
Sparse Core Ops, SparseCore 0:
  200.7 45.7 reduce-scatter.1
  248.5 24.9 all-gather.2
